TPU v7x, 512 devices: a whole 4x4x16 slice. The times are simulated.
512 devices in a mesh: nodes: 64 (over x, z), heads: 8 (over y, core).
Axes of the slice: x: 4, y: 4, z: 16, core: 2. Of those that a mesh axis runs over, the one named last changes fastest.
Arguments:
- hidden: bfloat16 [64, 7168], P('nodes'), may hold values from -6 to 6
- norm_gain: float32 [7168], replicated, may hold values from 0.1 to 1.9
- qkv_weight: bfloat16 [7168, 56, 384], P('nodes', 'heads'), may hold values from -0.0625 to 0.0625
- out_weight: bfloat16 [7168, 7168], P('heads', 'nodes'), may hold values from -0.0625 to 0.0625
- prefix_keys: bfloat16 [256, 128, 56, 128], P('nodes', None, 'heads'), may hold values from -1000 to 1000
- prefix_values: bfloat16 [256, 128, 56, 128], P('nodes', None, 'heads'), may hold values from -3 to 3
- leaf_keys: bfloat16 [64, 64, 56, 128], P('nodes', None, 'heads'), may hold values from -1000 to 1000
- leaf_values: bfloat16 [64, 64, 56, 128], P('nodes', None, 'heads'), may hold values from -3 to 3
- piece_node: int32 [256], replicated, may hold values from 0 to 35, as said below
- mid_parent: int32 [32], replicated, may hold values from 0 to 3
- leaf_parent: int32 [64], replicated, may hold values from 0 to 31
- leaf_len: int32 [64], replicated, may hold values from 1 to 64
- sink_len: int32 [64], replicated, may hold values from 0 to 4
- window_len: int32 [64], replicated, may hold values from 2048 to 4096
Outputs:
- layer_out: bfloat16 [64, 7168], P('heads', 'nodes')
Inputs may be any that keep to these rules, and one draw needn't show every extreme that they name: `piece_node`: every root owns some pieces; a middle node may own none.
All inputs are finite; a program needn't handle non-finite values.
Results may differ from a plain program's by a relative error of at most 0.007.
The roundings to bfloat16 on the way count: a program that leaves them out, or rounds other values in their place, can miss the bound.
Values may be sent and summed in bfloat16 or wider, within the bound.
A program may use at most 64 MiB of HBM per device.

v0:
```python
import math
import jax
import jax.numpy as jnp
from jax import lax
from jax.sharding import PartitionSpec as P

SEG = 128
ROOTS = 4
MIDS = 32
epsilon = 1e-05
negative_fill = -1e30


def joined(part, axis, combine):
    gathered = jax.tree.map(lambda a: lax.all_gather(a, axis), part)

    def take(source):
        return jax.tree.map(lambda a: lax.dynamic_index_in_dim(a, source, 0, False), gathered)

    return lax.fori_loop(
        1, lax.axis_size(axis), lambda source, state: combine(state, take(source)), take(0)
    )


def layer_norm(hidden, norm_gain):
    values = hidden.astype(jnp.float32)
    mean_value = jnp.mean(values, axis=1, keepdims=True)
    centered = values - mean_value
    variance = jnp.mean(centered * centered, axis=1, keepdims=True)
    return (centered * lax.rsqrt(variance + epsilon) * norm_gain[None, :]).astype(jnp.bfloat16)


def lookup(lookup_table, chosen):
    positions = jnp.arange(lookup_table.shape[0], dtype=jnp.int32)
    picked = jnp.where(chosen[:, None] == positions[None, :], lookup_table[None, :], 0)
    return jnp.sum(picked, axis=1)


def tree_rows(piece_node, mid_parent, leaf_parent, leaf_len):
    node_ids = jnp.arange(ROOTS + MIDS, dtype=jnp.int32)
    counts = jnp.sum((piece_node[:, None] == node_ids[None, :]).astype(jnp.int32), axis=0)
    root_node = lookup(mid_parent, leaf_parent)
    mid_node = leaf_parent + ROOTS
    root_len = SEG * lookup(counts, root_node)
    mid_len = SEG * lookup(counts, mid_node)
    finish = root_len + mid_len + leaf_len
    return (root_node, mid_node, root_len, finish)


def piece_rank(piece_node, chosen):
    all_pieces = jnp.arange(piece_node.shape[0], dtype=jnp.int32)
    nodes_here = lookup(piece_node, chosen)
    same = (piece_node[None, :] == nodes_here[:, None]) & (all_pieces[None, :] < chosen[:, None])
    return (nodes_here, jnp.sum(same.astype(jnp.int32), axis=1))


def prefix_allowed(
    node_block, rank_block, root_node, mid_node, root_len, finish, sink_len, window_len
):
    offsets = jnp.arange(SEG, dtype=jnp.int32)
    rel_pos = rank_block[:, None] * SEG + offsets[None, :]
    at_root = node_block[None, :] == root_node[:, None]
    at_mid = node_block[None, :] == mid_node[:, None]
    token_pos = rel_pos[None, :, :] + jnp.where(at_mid, root_len[:, None], 0)[:, :, None]
    inside = (token_pos < sink_len[:, None, None]) | (
        token_pos >= (finish - window_len)[:, None, None]
    )
    return ((at_root | at_mid)[:, :, None] & inside)[:, None, :, :]


def leaf_allowed(finish, leaf_len, sink_len, window_len, leaf_max):
    offsets = jnp.arange(leaf_max, dtype=jnp.int32)
    token_pos = (finish - leaf_len)[:, None] + offsets[None, :]
    inside = (token_pos < sink_len[:, None]) | (token_pos >= (finish - window_len)[:, None])
    return (inside & (offsets[None, :] < leaf_len[:, None]))[:, None, :]


def combine(first_part, second_part):
    highest = jnp.maximum(first_part[0], second_part[0])
    factor_one = jnp.exp(first_part[0] - highest)
    factor_two = jnp.exp(second_part[0] - highest)
    totals = first_part[1] * factor_one + second_part[1] * factor_two
    summed = first_part[2] * factor_one[..., None] + second_part[2] * factor_two[..., None]
    return (highest, totals, summed)


def weigh(scores, allowed, axes):
    masked = jnp.where(allowed, scores, negative_fill)
    maxima = jnp.max(masked, axis=axes)
    expanded = maxima
    for axis_pos in axes:
        expanded = jnp.expand_dims(expanded, axis_pos)
    weights = jnp.where(allowed, jnp.exp(masked - expanded), 0.0).astype(jnp.bfloat16)
    return (maxima, weights)


def on_device(
    hidden,
    norm_gain,
    qkv_weight,
    out_weight,
    prefix_keys,
    prefix_values,
    leaf_keys,
    leaf_values,
    piece_node,
    mid_parent,
    leaf_parent,
    leaf_len,
    sink_len,
    window_len,
):
    node_index = lax.axis_index("nodes")
    req_dev = hidden.shape[0]
    heads_dev = qkv_weight.shape[1]
    head_size = qkv_weight.shape[2] // 3
    seg_dev = prefix_keys.shape[0]
    first_row = node_index * req_dev
    score_scale = 1.0 / math.sqrt(head_size)
    normed = layer_norm(hidden, norm_gain)
    columns = lax.all_to_all(normed, "nodes", split_axis=1, concat_axis=0, tiled=True)
    width_here = columns.shape[1]
    flat_weight = qkv_weight.reshape(width_here, heads_dev * 3 * head_size)
    mixed_rows = lax.psum_scatter(
        jnp.dot(columns, flat_weight, preferred_element_type=jnp.float32),
        "nodes",
        scatter_dimension=0,
        tiled=True,
    )
    mixed_rows = mixed_rows.astype(jnp.bfloat16).reshape(req_dev, heads_dev, 3, head_size)
    query_here = mixed_rows[:, :, 0]
    key_new = mixed_rows[:, :, 1]
    value_new = mixed_rows[:, :, 2]
    query_all = lax.all_gather(query_here, "nodes", axis=0, tiled=True)
    root_node, mid_node, root_len, finish = tree_rows(piece_node, mid_parent, leaf_parent, leaf_len)
    chosen = node_index * seg_dev + jnp.arange(seg_dev, dtype=jnp.int32)
    node_block, rank_block = piece_rank(piece_node, chosen)
    scores = (
        jnp.einsum("rhd,pshd->rhps", query_all, prefix_keys, preferred_element_type=jnp.float32)
        * score_scale
    )
    allowed = prefix_allowed(
        node_block, rank_block, root_node, mid_node, root_len, finish, sink_len, window_len
    )
    maxima, weights = weigh(scores, allowed, (2, 3))
    totals = jnp.sum(weights.astype(jnp.float32), axis=(2, 3))
    summed = jnp.einsum(
        "rhps,pshd->rhd", weights, prefix_values, preferred_element_type=jnp.float32
    )
    merged = joined((maxima, totals, summed), "nodes", combine)
    merged = tuple((lax.dynamic_slice_in_dim(member, first_row, req_dev, 0) for member in merged))
    finish_here = lax.dynamic_slice_in_dim(finish, first_row, req_dev, 0)
    leaf_here = lax.dynamic_slice_in_dim(leaf_len, first_row, req_dev, 0)
    sink_here = lax.dynamic_slice_in_dim(sink_len, first_row, req_dev, 0)
    window_here = lax.dynamic_slice_in_dim(window_len, first_row, req_dev, 0)
    leaf_scores = (
        jnp.einsum("rhd,rjhd->rhj", query_here, leaf_keys, preferred_element_type=jnp.float32)
        * score_scale
    )
    leaf_mask = leaf_allowed(finish_here, leaf_here, sink_here, window_here, leaf_keys.shape[1])
    leaf_max, leaf_weights = weigh(leaf_scores, leaf_mask, (2,))
    leaf_part = (
        leaf_max,
        jnp.sum(leaf_weights.astype(jnp.float32), axis=2),
        jnp.einsum("rhj,rjhd->rhd", leaf_weights, leaf_values, preferred_element_type=jnp.float32),
    )
    own_score = (
        jnp.sum(query_here.astype(jnp.float32) * key_new.astype(jnp.float32), axis=2) * score_scale
    )
    own_part = (
        own_score,
        jnp.ones((req_dev, heads_dev), jnp.float32),
        value_new.astype(jnp.float32),
    )
    merged = combine(combine(merged, leaf_part), own_part)
    attended = (
        (merged[2] / merged[1][..., None])
        .astype(jnp.bfloat16)
        .reshape(req_dev, heads_dev * head_size)
    )
    out_rows = jnp.dot(
        lax.all_gather(attended, "nodes", axis=0, tiled=True),
        out_weight,
        preferred_element_type=jnp.float32,
    )
    return lax.psum_scatter(out_rows, "heads", scatter_dimension=0, tiled=True).astype(jnp.bfloat16)


def solution(mesh):
    return jax.shard_map(
        on_device,
        mesh=mesh,
        in_specs=(
            P("nodes", None),
            P(),
            P("nodes", "heads", None),
            P("heads", "nodes"),
            P("nodes", None, "heads", None),
            P("nodes", None, "heads", None),
            P("nodes", None, "heads", None),
            P("nodes", None, "heads", None),
            P(),
            P(),
            P(),
            P(),
            P(),
            P(),
        ),
        out_specs=P("heads", "nodes"),
        check_vma=False,
    )
```

profile of v0, /device:TPU:2, one launch (start us, length us, event | category | flops | bytes accessed | tf_op | source)
XLA Modules:
  0.0 810.2 jit_solution(8103925422148323476)
XLA Ops:
  6.5 1.5 convert_reduce_fusion.3
  8.7 1.4 multiply_reduce_fusion
  12.4 18.6 %all-to-all-start = ((bf16[1,64,112]{2,0,1:T(2,128)(2,1)}), bf16[1,64,112]{2,0,1:T(2,128)(2,1)S(1)}, u32[]{:S(2)}, u32[]{:S(2)}) async-start(bf16[1,64,112]{2,0,1:T(2,128)(2,1)} %all_to_all.15), calls=%async_computation | async-start | bytes 65536 | tf_op jit(solution)/shard_map/all_to_all | solution.py:121
  36.9 1.1 copy.86
  38.0 1.3 dynamic-slice
  39.3 5.2 all-to-all-done
  44.7 257.9 %all-reduce.3 = bf16[64,2688]{1,0:T(8,128)(2,1)S(1)} all-reduce(f32[64,2688]{1,0:T(8,128)S(1)} %fusion.19), channel_id=6, replica_groups=mesh['nodes'=64,'heads'=8] {'nodes'}, use_global_device_ids=true, to_apply=%region_8.9.clone | all-reduce | flops 172032 | bytes 1032192
  303.3 120.7 %all-gather = bf16[64,7,1,128]{3,1,2,0:T(8,128)(2,1)S(1)} all-gather(bf16[1,7,1,128]{3,1,2,0:T(8,128)(2,1)S(1)} %copy.68), channel_id=2, replica_groups=mesh['nodes'=64,'heads'=8] {'nodes'}, dimensions={0}, use_global_device_ids=true | all-gather | bytes 116480 | tf_op jit(solution)/shard_map/all_gather | solution.py:134
  424.5 2.2 convolution_bitcast_fusion
  426.8 1.2 dynamic_slice.68
  428.0 1.3 dynamic_slice.70
  429.3 1.3 dynamic_slice.69
  433.7 1.3 dynamic-slice.2
  435.7 1.3 compare_and_fusion
  437.0 78.9 %all-gather.4 = f32[64,64,7]{1,2,0:T(8,128)S(1)} all-gather(f32[1,64,7]{1,2,0:T(8,128)S(1)} %bitcast.134), channel_id=3, replica_groups=mesh['nodes'=64,'heads'=8] {'nodes'}, dimensions={0}, use_global_device_ids=true | all-gather | bytes 116480 | tf_op jit(solution)/shard_map/all_gather | solution.py:15
  516.2 82.0 %all-gather.5 = f32[64,64,7]{1,2,0:T(8,128)S(1)} all-gather(f32[1,64,7]{1,2,0:T(8,128)S(1)} %bitcast.136), channel_id=4, replica_groups=mesh['nodes'=64,'heads'=8] {'nodes'}, dimensions={0}, use_global_device_ids=true | all-gather | bytes 116480 | tf_op jit(solution)/shard_map/all_gather | solution.py:15
  598.2 1.1 fusion.16
  599.8 1.0 fusion.14
  602.3 95.5 %while.19 = (s32[]{:T(128)}, f32[64,7]{0,1:T(8,128)S(1)}, f32[64,7]{0,1:T(8,128)S(1)}, f32[64,7,128]{2,1,0:T(8,128)S(1)}, f32[64,64,7]{1,2,0:T(8,128)S(1)}, /*in...) while((s32[]{:T(128)}, f32[64,7]{0,1:T(8,128)S(1)}, ...), condition=%wide.region_12.13_spmd, body=%wide.region_11.12_spmd.sunk | while | flops 174725 | bytes 1172119 | solution.py:20
  603.8 1.0 constant_dynamic-slice_fusion.4
  606.9 1.0 constant_dynamic-slice_fusion.4
  609.9 1.0 constant_dynamic-slice_fusion.4
  612.9 1.0 constant_dynamic-slice_fusion.4
  615.9 1.0 constant_dynamic-slice_fusion.4
  619.0 1.0 constant_dynamic-slice_fusion.4
  623.5 1.0 constant_dynamic-slice_fusion.4
  626.6 1.0 constant_dynamic-slice_fusion.4
  629.6 1.0 constant_dynamic-slice_fusion.4
  632.6 1.0 constant_dynamic-slice_fusion.4
  635.7 1.0 constant_dynamic-slice_fusion.4
  638.7 1.0 constant_dynamic-slice_fusion.4
  641.7 1.0 constant_dynamic-slice_fusion.4
  644.7 1.0 constant_dynamic-slice_fusion.4
  647.8 1.0 constant_dynamic-slice_fusion.4
  652.3 1.0 constant_dynamic-slice_fusion.4
  655.4 1.0 constant_dynamic-slice_fusion.4
  658.4 1.0 constant_dynamic-slice_fusion.4
  661.4 1.0 constant_dynamic-slice_fusion.4
  664.5 1.0 constant_dynamic-slice_fusion.4
  667.5 1.0 constant_dynamic-slice_fusion.4
  670.5 1.0 constant_dynamic-slice_fusion.4
  673.5 1.0 constant_dynamic-slice_fusion.4
  676.6 1.0 constant_dynamic-slice_fusion.4
  681.1 1.0 constant_dynamic-slice_fusion.4
  684.2 1.0 constant_dynamic-slice_fusion.4
  687.2 1.0 constant_dynamic-slice_fusion.4
  698.2 80.7 %all-gather.6 = bf16[64,1,896]{2,1,0:T(2,128)(2,1)S(1)} all-gather(bf16[1,1,896]{2,1,0:T(2,128)(2,1)S(1)} %convert_bitcast_fusion), channel_id=1, replica_groups=mesh['nodes'=64,'heads'=8] {'nodes'}, dimensions={0}, use_global_device_ids=true | all-gather | bytes 116480 | tf_op jit(solution)/shard_map/all_gather | solution.py:182
  779.1 23.6 %all-reduce.1 = bf16[64,112]{1,0:T(8,128)(2,1)S(1)} all-reduce(f32[64,112]{1,0:T(8,128)S(1)} %fusion.10), channel_id=7, replica_groups=mesh['nodes'=64,'heads'=8] {'heads'}, use_global_device_ids=true, to_apply=%region_16.17.clone | all-reduce | flops 7168 | bytes 43008
  (334 shorter events, 80.1 us)
Async XLA Ops:
  6.5 417.5 %copy-start = (bf16[4,128,7,128]{3,1,2,0:T(8,128)(2,1)S(1)}, bf16[4,128,7,128]{3,1,2,0:T(8,128)(2,1)}, u32[]{:S(2)}) copy-start(bf16[4,128,7,128]{3,1,2,0:T(8,128)(2,1)} %param.20) | copy-start | bytes 2752516
  6.5 772.4 %copy-start.1 = (bf16[896,112]{0,1:T(8,128)(2,1)S(1)}, bf16[896,112]{0,1:T(8,128)(2,1)}, u32[]{:S(2)}) copy-start(bf16[896,112]{0,1:T(8,128)(2,1)} %param.19) | copy-start | bytes 602116
  12.4 32.1 %all-to-all-start = ((bf16[1,64,112]{2,0,1:T(2,128)(2,1)}), bf16[1,64,112]{2,0,1:T(2,128)(2,1)S(1)}, u32[]{:S(2)}, u32[]{:S(2)}) async-start(bf16[1,64,112]{2,0,1:T(2,128)(2,1)} %all_to_all.15), calls=%async_computation | async-start | bytes 65536 | tf_op jit(solution)/shard_map/all_to_all | solution.py:121
  31.0 570.1 %all-gather.9.cloned.1.call-start = ((), (), s32[]{:S(2)}) async-start(), calls=%async_computation.1 | async-start | bytes 14909440 | tf_op jit(solution)/shard_map/all_gather | solution.py:15
Sparse Core Ops, SparseCore 0:
  426.9 174.2 all-gather.8
where the time goes:
time: 813 us; the launch traced here: 810 us
  blocking collectives  644 us (79%)
  local copies, waits for them, and re-layouts  84.4 us (10%)
  other arithmetic  32.2 us (4%)
  starting transfers between devices  18.7 us (2%)
  between operations  18 us (2%)
    unnamed x2, blocking collectives  281 us
    all_gather x2, blocking collectives, joined(): gathered = jax.tree.map(lambda a: lax.all_gather(a, axis), part)  161 us
    all_gather x1, blocking collectives, on_device(): query_all = lax.all_gather(query_here, 'nodes', axis=0, tiled=True)  121 us
    all_gather x1, blocking collectives, on_device(): lax.all_gather(attended, 'nodes', axis=0, tiled=True)  80.7 us
    dynamic_slice x66, local copies, waits for them, and re-layouts, take(): lax.dynamic_index_in_dim(a, source, 0, False)  61.8 us
    add x63, other arithmetic, combine(): first_part[2] * factor_one[..., None]  19.3 us
    all_to_all x1, starting transfers between devices, on_device(): lax.all_to_all(normed, 'nodes', split_axis=1, concat_axis=0, tiled=True)  18.6 us
  transfers between devices with their start and end apart: 2, of which 2 were waited for; matrix products, arithmetic and copies ran while one was open for 2% of the time, Pallas kernels for 0%

commit v1 on v0

--- a/solution.py
+++ b/solution.py
@@ -9,6 +9,13 @@
 MIDS = 32
 epsilon = 1e-05
 negative_fill = -1e30
+
+
+def stacked_exchange(x, name, split, join):
+    peers = lax.axis_size(name)
+    blocks = jnp.stack(jnp.split(x, peers, axis=split), axis=0)
+    blocks = lax.all_to_all(blocks, name, split_axis=0, concat_axis=0)
+    return jnp.concatenate(blocks, axis=join)
 
 
 def joined(part, axis, combine):
@@ -118,7 +125,7 @@
     first_row = node_index * req_dev
     score_scale = 1.0 / math.sqrt(head_size)
     normed = layer_norm(hidden, norm_gain)
-    columns = lax.all_to_all(normed, "nodes", split_axis=1, concat_axis=0, tiled=True)
+    columns = stacked_exchange(normed, "nodes", 1, 0)
     width_here = columns.shape[1]
     flat_weight = qkv_weight.reshape(width_here, heads_dev * 3 * head_size)
     mixed_rows = lax.psum_scatter(

time: 813 us -> 851 us (1.047)
  local copies, waits for them, and re-layouts: 84.4 us -> 123 us
    unnamed x6 -> x69, local copies, waits for them, and re-layouts: 2.6 us -> 40.7 us
where the time goes in v1:
time: 851 us; the launch traced here: 848 us
  blocking collectives  644 us (76%)
  local copies, waits for them, and re-layouts  123 us (14%)
  other arithmetic  32.3 us (4%)
  starting transfers between devices  18.7 us (2%)
  between operations  18 us (2%)
    unnamed x2, blocking collectives  281 us
    all_gather x2, blocking collectives, joined(): gathered = jax.tree.map(lambda a: lax.all_gather(a, axis), part)  161 us
    all_gather x1, blocking collectives, on_device(): query_all = lax.all_gather(query_here, 'nodes', axis=0, tiled=True)  121 us
    all_gather x1, blocking collectives, on_device(): lax.all_gather(attended, 'nodes', axis=0, tiled=True)  80.7 us
    dynamic_slice x66, local copies, waits for them, and re-layouts, take(): lax.dynamic_index_in_dim(a, source, 0, False)  61.8 us
    unnamed x69, local copies, waits for them, and re-layouts  40.7 us
    add x63, other arithmetic, combine(): first_part[2] * factor_one[..., None]  19.3 us
    all_to_all x1, starting transfers between devices, stacked_exchange(): blocks = lax.all_to_all(blocks, name, split_axis=0, concat_axis=0)  18.6 us
  transfers between devices with their start and end apart: 2, of which 2 were waited for; matrix products, arithmetic and copies ran while one was open for 2% of the time, Pallas kernels for 0%

profile of v1, /device:TPU:2, one launch (start us, length us, event | category | flops | bytes accessed | tf_op | source)
XLA Modules:
  0.0 848.4 jit_solution(3173547713119589487)
XLA Ops:
  6.5 1.5 convert_reduce_fusion.2
  8.7 1.4 multiply_reduce_fusion
  50.5 18.6 %all-to-all-start = ((bf16[64,1,112]{2,1,0:T(2,128)(2,1)}), bf16[64,1,112]{2,1,0:T(2,128)(2,1)S(1)}, u32[]{:S(2)}, u32[]{:S(2)}) async-start(bf16[64,1,112]{2,1,0:T(2,128)(2,1)} %constant_dynamic-update-slice_fusion), calls=%async_computation | async-start | bytes 65536 | tf_op jit(solution)/shard_map/all_to_all | solution.py:17
  74.9 1.1 copy.72
  76.1 1.3 dynamic-slice
  77.3 5.2 all-to-all-done
  82.8 257.9 %all-reduce.3 = bf16[64,2688]{1,0:T(8,128)(2,1)S(1)} all-reduce(f32[64,2688]{1,0:T(8,128)S(1)} %fusion.19), channel_id=6, replica_groups=mesh['nodes'=64,'heads'=8] {'nodes'}, use_global_device_ids=true, to_apply=%region_8.9.clone | all-reduce | flops 172032 | bytes 1032192
  341.4 120.7 %all-gather = bf16[64,7,1,128]{3,1,2,0:T(8,128)(2,1)S(1)} all-gather(bf16[1,7,1,128]{3,1,2,0:T(8,128)(2,1)S(1)} %copy.54), channel_id=2, replica_groups=mesh['nodes'=64,'heads'=8] {'nodes'}, dimensions={0}, use_global_device_ids=true | all-gather | bytes 116480 | tf_op jit(solution)/shard_map/all_gather | solution.py:141
  462.6 2.2 convolution_bitcast_fusion
  464.9 1.2 dynamic_slice.68
  466.1 1.3 dynamic_slice.70
  467.4 1.3 dynamic_slice.69
  471.8 1.3 dynamic-slice.2
  473.7 1.3 compare_and_fusion
  475.1 78.9 %all-gather.4 = f32[64,64,7]{1,2,0:T(8,128)S(1)} all-gather(f32[1,64,7]{1,2,0:T(8,128)S(1)} %bitcast.390), channel_id=3, replica_groups=mesh['nodes'=64,'heads'=8] {'nodes'}, dimensions={0}, use_global_device_ids=true | all-gather | bytes 116480 | tf_op jit(solution)/shard_map/all_gather | solution.py:22
  554.3 82.0 %all-gather.5 = f32[64,64,7]{1,2,0:T(8,128)S(1)} all-gather(f32[1,64,7]{1,2,0:T(8,128)S(1)} %bitcast.392), channel_id=4, replica_groups=mesh['nodes'=64,'heads'=8] {'nodes'}, dimensions={0}, use_global_device_ids=true | all-gather | bytes 116480 | tf_op jit(solution)/shard_map/all_gather | solution.py:22
  636.3 1.1 fusion.16
  637.9 1.0 fusion.14
  640.3 95.6 %while.19 = (s32[]{:T(128)}, f32[64,7]{0,1:T(8,128)S(1)}, f32[64,7]{0,1:T(8,128)S(1)}, f32[64,7,128]{2,1,0:T(8,128)S(1)}, f32[64,64,7]{1,2,0:T(8,128)S(1)}, /*in...) while((s32[]{:T(128)}, f32[64,7]{0,1:T(8,128)S(1)}, ...), condition=%wide.region_12.13_spmd, body=%wide.region_11.12_spmd.sunk | while | flops 174725 | bytes 1172119 | solution.py:27
  640.4 1.0 constant_dynamic-slice_fusion.4
  644.9 1.0 constant_dynamic-slice_fusion.4
  646.5 1.0 constant_dynamic-slice_fusion.4
  651.0 1.0 constant_dynamic-slice_fusion.4
  655.6 1.0 constant_dynamic-slice_fusion.4
  657.1 1.0 constant_dynamic-slice_fusion.4
  661.6 1.0 constant_dynamic-slice_fusion.4
  663.2 1.0 constant_dynamic-slice_fusion.4
  667.7 1.0 constant_dynamic-slice_fusion.4
  669.2 1.0 constant_dynamic-slice_fusion.4
  673.8 1.0 constant_dynamic-slice_fusion.4
  675.3 1.0 constant_dynamic-slice_fusion.4
  679.9 1.0 constant_dynamic-slice_fusion.4
  684.4 1.0 constant_dynamic-slice_fusion.4
  685.9 1.0 constant_dynamic-slice_fusion.4
  690.5 1.0 constant_dynamic-slice_fusion.4
  692.0 1.0 constant_dynamic-slice_fusion.4
  696.6 1.0 constant_dynamic-slice_fusion.4
  698.1 1.0 constant_dynamic-slice_fusion.4
  702.6 1.0 constant_dynamic-slice_fusion.4
  704.1 1.0 constant_dynamic-slice_fusion.4
  708.7 1.0 constant_dynamic-slice_fusion.4
  713.2 1.0 constant_dynamic-slice_fusion.4
  714.8 1.0 constant_dynamic-slice_fusion.4
  719.3 1.0 constant_dynamic-slice_fusion.4
  720.8 1.0 constant_dynamic-slice_fusion.4
  725.4 1.0 constant_dynamic-slice_fusion.4
  736.4 80.7 %all-gather.6 = bf16[64,1,896]{2,1,0:T(2,128)(2,1)S(1)} all-gather(bf16[1,1,896]{2,1,0:T(2,128)(2,1)S(1)} %convert_bitcast_fusion), channel_id=1, replica_groups=mesh['nodes'=64,'heads'=8] {'nodes'}, dimensions={0}, use_global_device_ids=true | all-gather | bytes 116480 | tf_op jit(solution)/shard_map/all_gather | solution.py:189
  817.3 23.6 %all-reduce.1 = bf16[64,112]{1,0:T(8,128)(2,1)S(1)} all-reduce(f32[64,112]{1,0:T(8,128)S(1)} %fusion.10), channel_id=7, replica_groups=mesh['nodes'=64,'heads'=8] {'heads'}, use_global_device_ids=true, to_apply=%region_16.17.clone | all-reduce | flops 7168 | bytes 43008
  (397 shorter events, 118.2 us)
Async XLA Ops:
  6.5 455.5 %copy-start = (bf16[4,128,7,128]{3,1,2,0:T(8,128)(2,1)S(1)}, bf16[4,128,7,128]{3,1,2,0:T(8,128)(2,1)}, u32[]{:S(2)}) copy-start(bf16[4,128,7,128]{3,1,2,0:T(8,128)(2,1)} %param.20) | copy-start | bytes 2752516
  6.5 810.6 %copy-start.1 = (bf16[896,112]{0,1:T(8,128)(2,1)S(1)}, bf16[896,112]{0,1:T(8,128)(2,1)}, u32[]{:S(2)}) copy-start(bf16[896,112]{0,1:T(8,128)(2,1)} %param.19) | copy-start | bytes 602116
  50.5 32.1 %all-to-all-start = ((bf16[64,1,112]{2,1,0:T(2,128)(2,1)}), bf16[64,1,112]{2,1,0:T(2,128)(2,1)S(1)}, u32[]{:S(2)}, u32[]{:S(2)}) async-start(bf16[64,1,112]{2,1,0:T(2,128)(2,1)} %constant_dynamic-update-slice_fusion), calls=%async_computation | async-start | bytes 65536 | tf_op jit(solution)/shard_map/all_to_all | solution.py:17
  69.1 570.1 %all-gather.9.cloned.1.call-start = ((), (), s32[]{:S(2)}) async-start(), calls=%async_computation.1 | async-start | bytes 14909440 | tf_op jit(solution)/shard_map/all_gather | solution.py:22
Sparse Core Ops, SparseCore 0:
  465.0 174.2 all-gather.8
